TPU v7x, 32 devices: a whole 2x2x4 slice. The times are simulated.
32 devices in a mesh: seq: 8 (over z, y), tp: 4 (over x, core).
Axes of the slice: x: 2, y: 2, z: 4, core: 2. Of those that a mesh axis runs over, the one named last changes fastest.
Arguments:
- queries: bfloat16 [768, 4096], P('seq', 'tp'), may hold values from -8 to 8
- keys: bfloat16 [768, 1024], P('seq', 'tp'), may hold values from -7 to 7
- values: bfloat16 [768, 1024], P('seq', 'tp'), may hold values from -24 to 24
- router_prob: float32 [768], P('seq'), may hold values from 0.2 to 1
- norm_gain: float32 [4096], P('tp'), may hold values from 0.25 to 1.75
- slot_pos: int32 [768], P('seq'), may hold values from 0 to 255, as said below
- live_count: int32 [8], P('seq'), may hold values from 1 to 96, 256 in all
Outputs:
- routed: bfloat16 [2048, 4096], P('seq', 'tp')
Inputs may be any that keep to these rules, and one draw needn't show every extreme that they name: The slots of a shard that are live are its first live_count slots; the counts add up to 256 and the largest is 96. Within each shard's 96 slots the positions are distinct and ascending; slot a of shard s stands for the token s * 256 + slot_pos[a].
All inputs are finite; a program needn't handle non-finite values.
Results may differ from a plain program's by a relative error of at most 0.007.
Values may be sent and summed in bfloat16 or wider, within the bound.
A program may use at most 64 MiB of HBM per device.

v0:
```python
import math

import jax
import jax.numpy as jnp
from jax import lax
from jax.sharding import PartitionSpec as P

H = 32
HD = 128
TOK_DEV = 256


far_number = 1 << 30
epsilon = 1e-06
block_limit = 1024
lowest = -1e30


def attend_block(
    carried,
    current_key_block,
    value_block,
    key_numbers,
    head_grouped_rows,
    query_numbers,
    score_scale,
):
    highest, totals, running_output = carried
    scores = (
        jnp.einsum(
            "zpeo,jpo->pezj",
            head_grouped_rows,
            current_key_block,
            preferred_element_type=jnp.float32,
        )
        * score_scale
    )
    visible = key_numbers[None, None, None, :] <= query_numbers[None, None, :, None]
    masked = jnp.where(visible, scores, lowest)
    newest = jnp.maximum(highest, jnp.max(masked, axis=-1))
    weights = jnp.where(visible, jnp.exp(scores - newest[..., None]), 0.0)
    factor = jnp.exp(highest - newest)
    totals = totals * factor + jnp.sum(weights, axis=-1)
    update = jnp.einsum(
        "ycwh,hyu->ycwu",
        weights.astype(jnp.bfloat16),
        value_block,
        preferred_element_type=jnp.float32,
    )
    running_output = running_output * factor[..., None] + update
    return (newest, totals, running_output)


def fold_blocks(
    carried, key_all, value_all, head_grouped_rows, query_numbers, number_rule, score_scale
):
    length = key_all.shape[0]
    block_rows = min(length, block_limit)
    block_count = -(-length // block_rows)
    offsets = jnp.arange(block_count * block_rows, dtype=jnp.int32)
    numbers = jnp.where(offsets < length, number_rule(offsets), far_number)
    count_of_heads = key_all.shape[1] // HD
    key_blocks = key_all.reshape(block_count, block_rows, count_of_heads, HD)
    value_blocks = value_all.reshape(block_count, block_rows, count_of_heads, HD)
    total_block_count = numbers.reshape(block_count, block_rows)
    newest_query = jnp.max(query_numbers)

    def advance(running, blocks):
        current_key_block, value_block, key_numbers = blocks

        def unchanged(inside):
            return inside

        def updated(inside):
            return attend_block(
                inside,
                current_key_block,
                value_block,
                key_numbers,
                head_grouped_rows,
                query_numbers,
                score_scale,
            )

        running = lax.cond(jnp.min(key_numbers) > newest_query, unchanged, updated, running)
        return (running, None)

    carried, ignored = lax.scan(advance, carried, (key_blocks, value_blocks, total_block_count))
    return carried


def local(queries, keys, values, router_prob, norm_gain, slot_pos, live_count):
    device_mesh = lax.axis_size("seq")
    my_index = lax.axis_index("seq")
    capacity = queries.shape[0]
    local_heads = queries.shape[1] // HD
    local_groups = keys.shape[1] // HD
    group_size = local_heads // local_groups
    score_scale = 1.0 / math.sqrt(HD)
    counts = lax.all_gather(live_count, "seq", axis=0, tiled=True)
    limits = jnp.cumsum(counts)
    starts = limits - counts
    shard_range = jnp.arange(device_mesh, dtype=jnp.int32)
    self_hot = shard_range == my_index
    start_here = jnp.sum(jnp.where(self_hot, starts, 0))
    count_here = jnp.sum(jnp.where(self_hot, counts, 0))
    slot_index = jnp.arange(capacity, dtype=jnp.int32)

    def slot_numbers(positions):
        shard_id = positions // capacity
        within = positions % capacity
        one_hot = shard_id[:, None] == shard_range[None, :]
        begins = jnp.sum(jnp.where(one_hot, starts[None, :], 0), axis=1)
        surviving_token_count = jnp.sum(jnp.where(one_hot, counts[None, :], 0), axis=1)
        return jnp.where(within < surviving_token_count, begins + within, far_number)

    query_numbers = start_here + jnp.minimum(slot_index, count_here - 1)
    row_count = queries.shape[0]
    head_grouped_rows = queries.reshape(row_count, local_groups, group_size, HD)
    initial = (
        jnp.full((local_groups, group_size, row_count), lowest, jnp.float32),
        jnp.zeros((local_groups, group_size, row_count), jnp.float32),
        jnp.zeros((local_groups, group_size, row_count, HD), jnp.float32),
    )
    key_all, value_all = (
        lax.all_gather(keys, "seq", axis=0, tiled=True),
        lax.all_gather(values, "seq", axis=0, tiled=True),
    )
    highest, totals, running_output = fold_blocks(
        initial, key_all, value_all, head_grouped_rows, query_numbers, slot_numbers, score_scale
    )
    attended = (running_output / totals[..., None]).astype(jnp.bfloat16)
    attended = jnp.transpose(attended, (2, 0, 1, 3)).reshape(row_count, local_heads * HD)
    widened = attended.astype(jnp.float32)
    squares = jnp.sum(widened * widened, axis=1)
    total_squares = lax.psum(squares, "tp")
    inverse = lax.rsqrt(total_squares / (H * HD) + epsilon)
    normed = (router_prob[:, None] * norm_gain[None, :] * widened * inverse[:, None]).astype(
        jnp.bfloat16
    )
    alive = slot_index < count_here
    placer = (
        (jnp.arange(TOK_DEV, dtype=jnp.int32)[:, None] == slot_pos[None, :]) & alive[None, :]
    ).astype(jnp.bfloat16)
    return jnp.dot(placer, normed, preferred_element_type=jnp.float32).astype(jnp.bfloat16)


def solution(mesh):
    in_specs = (
        P("seq", "tp"),
        P("seq", "tp"),
        P("seq", "tp"),
        P("seq"),
        P("tp"),
        P("seq"),
        P("seq"),
    )
    out_specs = P("seq", "tp")
    return jax.shard_map(local, mesh=mesh, in_specs=in_specs, out_specs=out_specs, check_vma=False)
```

profile of v0, /device:TPU:0, one launch (start us, length us, event | category | flops | bytes accessed | tf_op | source)
XLA Modules:
  0.0 98.1 jit_solution(10348603739247886272)
XLA Ops:
  0.7 1.2 %dynamic-slice.1 = u32[1]{0:T(128)} dynamic-slice(u32[32]{0:T(128)} %constant.81, u32[]{:T(128)S(6)} %add.49), dynamic_slice_sizes={1} | dynamic-slice | bytes 12
  1.9 0.8 dynamic-update-slice
  2.7 13.1 %all-reduce = s32[8]{0:T(128)S(1)} all-reduce(s32[8]{0:T(128)S(1)} %dynamic-update-slice), channel_id=1, replica_groups=mesh['seq'=8,'tp'=4] {'seq'}, use_global_device_ids=true, to_apply=%add | all-reduce | flops 8 | bytes 64
  15.8 0.2 reduce-window.9
  15.9 0.6 fusion.31
  16.6 0.1 select_reduce_fusion.1
  16.7 0.7 fusion.33
  18.0 1.3 %fusion.32 = (s32[]{:T(128)}, s32[96]{0:T(128)S(1)}) fusion(s32[]{:T(128)S(6)} %sub.33, s32[]{:T(128)} %get-tuple-element.108), kind=kLoop, calls=%fused_computation.59 | loop fusion | flops 287 | bytes 396 | tf_op jit(solution)/shard_map/reduce_max | solution.py:66
  20.6 31.4 %all_gather.10 = bf16[768,256]{1,0:T(8,128)(2,1)S(1)} all-gather(bf16[96,256]{1,0:T(8,128)(2,1)} %param.10), channel_id=1, replica_groups=mesh['seq'=8,'tp'=4] {'seq'}, dimensions={0}, use_global_device_ids=true | all-gather | bytes 442368 | tf_op jit(solution)/shard_map/all_gather | solution.py:126
  51.9 31.2 %all_gather.11 = bf16[768,256]{1,0:T(8,128)(2,1)S(1)} all-gather(bf16[96,256]{1,0:T(8,128)(2,1)} %param.11), channel_id=1, replica_groups=mesh['seq'=8,'tp'=4] {'seq'}, dimensions={0}, use_global_device_ids=true | all-gather | bytes 442368 | tf_op jit(solution)/shard_map/all_gather | solution.py:127
  83.1 6.7 %conditional.1 = ((f32[2,4,96]{2,1,0:T(4,128)S(1)}, f32[2,4,96,128]{3,2,1,0:T(8,128)S(1)})) conditional(s32[]{:T(128)} %convert_element_type.32, (s32[768]{0:T(1024)S(1)}, s32[96]{0:T(128)S(1)}, bf16[768,256]{1,0:T(8,128)(2,1)S(1)}, bf16[96,1024]{1,0:T(8,128)(2,1)}, f32[2,4,96]{2,1,0:T(4,128)S(1)}, /*index=5*/f32[2,4,96,128]{3,2,1,0:T(8,128)S(1)}, ...), branch_computations={%region_7.10_spmd, %region_10.11_spmd} | conditional | flops 308750592 | bytes 11443636 | solution.py:85
  83.1 0.7 broadcast_compare_fusion
  83.9 1.7 %reshape.96 = bf16[96,2,4,128]{3,2,1,0:T(4,128)(2,1)} reshape(bf16[96,1024]{1,0:T(8,128)(2,1)} %get-tuple-element.101) | data formatting | bytes 393216 | tf_op jit(solution)/shard_map/reshape | solution.py:119
  85.6 0.1 squeeze.14
  85.7 1.7 %fusion = (f32[2,4,96]{2,1,0:T(4,128)S(1)}, f32[2,768,96,4]{1,2,3,0:T(8,128)S(1)}) fusion(pred[96,768]{1,0:T(8,128)(4,1)} %broadcast_compare_fusion, bf16[96,2,4,128]{3,2,1,0:T(4,128)(2,1)} %reshape.96, bf16[768,2,128,1]{2,1,0,3:T(2,128)(2,1)S(1)} %bitcast.24), kind=kOutput, calls=%fused_computation.2 | convolution fusion | flops 152763648 | bytes 3025920 | tf_op jit(solution)/shard_map/while/body/eval_jaxpr/cond/branch_0_fun/zpeo,jpo->pezj/dot_general | solution.py:30
  87.4 0.7 fusion.4
  88.1 0.1 squeeze.15
  88.2 1.6 %convolution_add_fusion = f32[2,4,96,128]{3,2,1,0:T(8,128)S(1)} fusion(f32[2,768,96,4]{1,2,3,0:T(8,128)S(1)} %get-tuple-element.115, f32[2,4,96]{2,1,0:T(4,128)S(1)} %broadcast_maximum_fusion, pred[96,768]{1,0:T(8,128)(4,1)} %broadcast_compare_fusion, bf16[768,2,128,1]{2,1,0,3:T(2,128)(2,1)S(1)} %bitcast.23, f32[2,4,96,128]{3,2,1,0:T(8,128)S(1)} %get-tuple-element.94, ...), kind=kOutput, calls=%fused_computation.7 | convolution fusion | flops 153550848 | bytes 3618816 | tf_op jit(solution)/shard_map/while/body/eval_jaxpr/cond/branch_0_fun/ycwh,hyu->ycwu/dot_general | solution.py:44
  89.9 0.3 fusion.16
  90.2 0.3 copy.19
  90.4 0.2 reshape.101
  90.6 5.7 %psum.7 = f32[96]{0:T(128)S(1)} all-reduce(f32[96]{0:T(128)S(1)} %get-tuple-element.104), channel_id=1, replica_groups=mesh['seq'=8,'tp'=4] {'tp'}, use_global_device_ids=true, to_apply=%region_12.13 | all-reduce | flops 96 | bytes 768 | tf_op jit(solution)/shard_map/psum | solution.py:136
  96.3 0.6 iota_compare_fusion.3
  97.0 1.2 %convolution_convert_fusion = bf16[256,1024]{1,0:T(8,128)(2,1)} fusion(f32[96,1024]{1,0:T(8,128)S(1)} %reshape.101, f32[96]{0:T(128)S(1)} %add_rsqrt_fusion, f32[1024]{0:T(1024)S(1)} %copy-done.1, f32[96]{0:T(128)S(1)} %copy-done.2, s32[96]{0:T(128)S(1)} %copy-done.3, pred[96]{0:T(512)(128)(4,1)S(1)} %iota_compare_fusion.3), kind=kOutput, calls=%fused_computation.22 | convolution fusion | flops 51036160 | bytes 922848 | tf_op jit(solution)/shard_map/dot_general | solution.py:145
  (16 shorter events, 0.1 us)
Async XLA Ops:
  85.7 1.7 %copy-start = (pred[96,768]{1,0:T(8,128)(4,1)S(1)}, pred[96,768]{1,0:T(8,128)(4,1)}, u32[]{:S(2)}) copy-start(pred[96,768]{1,0:T(8,128)(4,1)} %broadcast_compare_fusion) | copy-start | bytes 221188 | tf_op jit(solution)/shard_map/while/body/eval_jaxpr/cond
  89.8 7.1 %copy-start.1 = (f32[1024]{0:T(1024)S(1)}, f32[1024]{0:T(1024)}, u32[]{:S(2)}) copy-start(f32[1024]{0:T(1024)} %param.13) | copy-start | bytes 12292
  89.9 7.1 %copy-start.2 = (f32[96]{0:T(128)S(1)}, f32[96]{0:T(128)}, u32[]{:S(2)}) copy-start(f32[96]{0:T(128)} %param.12) | copy-start | bytes 1156
  89.9 7.1 %copy-start.3 = (s32[96]{0:T(128)S(1)}, s32[96]{0:T(128)}, u32[]{:S(2)}) copy-start(s32[96]{0:T(128)} %param.14) | copy-start | bytes 1156
where the time goes:
time: 98.4 us; the launch traced here: 98.1 us
  blocking collectives  81.3 us (83%)
  other arithmetic  5.32 us (5%)
  matrix products  4.44 us (5%)
  local copies, waits for them, and re-layouts  4.37 us (4%)
  between operations  2.64 us (3%)
    all_gather x1, blocking collectives, local(): lax.all_gather(keys, 'seq', axis=0, tiled=True)  31.4 us
    all_gather x1, blocking collectives, local(): lax.all_gather(values, 'seq', axis=0, tiled=True)  31.2 us
    unnamed x1, blocking collectives  13.1 us
    psum x1, blocking collectives, local(): total_squares = lax.psum(squares, 'tp')  5.67 us
    unnamed x9, local copies, waits for them, and re-layouts  2.02 us

commit v1 on v0

--- a/solution.py
+++ b/solution.py
@@ -1,8 +1,11 @@
+import functools
 import math
 
 import jax
 import jax.numpy as jnp
 from jax import lax
+from jax.experimental import pallas as pl
+from jax.experimental.pallas import tpu as pltpu
 from jax.sharding import PartitionSpec as P
 
 H = 32
@@ -145,6 +148,321 @@
     return jnp.dot(placer, normed, preferred_element_type=jnp.float32).astype(jnp.bfloat16)
 
 
+WIDTH = 2
+KERNEL_SHARDS = 16
+MESH = pl.DeviceIdType.MESH
+FLAT = (((1,), (1,)), ((), ()))
+TALL = (((0,), (0,)), ((), ()))
+
+
+def kernel(
+    shards,
+    tp_size,
+    q_hbm,
+    k_hbm,
+    v_hbm,
+    prob_ref,
+    gain_ref,
+    pos_ref,
+    count_ref,
+    out_ref,
+    q_buf,
+    k_buf,
+    v_buf,
+    count_buf,
+    high_ref,
+    total_ref,
+    acc_ref,
+    att_ref,
+    placed_ref,
+    square_out,
+    square_in,
+    local_sem,
+    send_sem,
+    recv_sem,
+    tp_send_sem,
+    tp_recv_sem,
+):
+    me = lax.axis_index("seq")
+    tp_me = lax.axis_index("tp")
+    rows = shards // WIDTH
+    row, column = me // WIDTH, lax.rem(me, WIDTH)
+    beside = me + 1 - 2 * column
+    groups, stacked, _ = q_buf.shape
+    capacity = k_buf.shape[1]
+    heads = stacked // capacity
+    rate = math.log2(math.e) / math.sqrt(HD)
+
+    local_copies = [
+        pltpu.make_async_copy(k_hbm, k_buf.at[me], local_sem.at[0]),
+        pltpu.make_async_copy(v_hbm, v_buf.at[me], local_sem.at[1]),
+    ]
+    for g in range(groups):
+        for h in range(heads):
+            local_copies.append(
+                pltpu.make_async_copy(
+                    q_hbm.at[:, pl.ds((g * heads + h) * HD, HD)],
+                    q_buf.at[g, pl.ds(h * capacity, capacity), :],
+                    local_sem.at[2 + g * heads + h],
+                )
+            )
+    for copy in local_copies:
+        copy.start()
+    my_count = count_ref[0]
+    count_buf[me] = jnp.full(count_buf.shape[1:], my_count, jnp.int32)
+    square_out[...] = jnp.zeros_like(square_out)
+
+    barrier = pltpu.get_barrier_semaphore()
+
+    def greet(**where):
+        pl.semaphore_signal(barrier, inc=1, device_id=where, device_id_type=MESH)
+
+    greet(seq=beside)
+    for step in range(1, tp_size):
+        greet(tp=lax.rem(tp_me + step, tp_size))
+
+    @pl.when(row > 0)
+    def _():
+        greet(seq=me - WIDTH)
+
+    @pl.when(row < rows - 1)
+    def _():
+        greet(seq=me + WIDTH)
+
+    pl.semaphore_wait(
+        barrier,
+        tp_size + jnp.where(row > 0, 1, 0) + jnp.where(row < rows - 1, 1, 0),
+    )
+
+    def piece_copy(kind, piece, way, back):
+        buffer = (k_buf, v_buf, count_buf)[kind]
+        source = buffer.at[piece]
+        if back == 0 and kind < 2:
+            source = (k_hbm, v_hbm)[kind]
+        return pltpu.make_async_remote_copy(
+            src_ref=source,
+            dst_ref=buffer.at[piece],
+            send_sem=send_sem.at[way, back, kind],
+            recv_sem=recv_sem.at[piece, kind],
+            device_id={"seq": (me + WIDTH, beside)[way]},
+            device_id_type=MESH,
+        )
+
+    def send_piece(kinds, back, act):
+        piece = me - WIDTH * back
+
+        @pl.when(row < rows - 1)
+        def _():
+            for kind in kinds:
+                act(piece_copy(kind, piece, 0, back))
+
+        if back == 0:
+
+            @pl.when(column == 0)
+            def _():
+                for kind in kinds:
+                    act(piece_copy(kind, piece, 1, back))
+        else:
+            for kind in kinds:
+                act(piece_copy(kind, piece, 1, back))
+
+    def await_piece(piece, kinds):
+        for kind in kinds:
+            piece_copy(kind, piece, 0, 1).wait_recv()
+
+    send_piece((2, 0, 1), 0, lambda copy: copy.start())
+
+    def attend(keys, values, visible, first):
+        for g in range(groups):
+            lanes = slice(g * HD, (g + 1) * HD)
+            scores = lax.dot_general(
+                keys[:, lanes], q_buf[g], FLAT, preferred_element_type=jnp.float32
+            )
+            scores = jnp.where(visible, scores, lowest)
+            newest = jnp.max(scores, axis=0, keepdims=True)
+            if not first:
+                highest = high_ref[g]
+                newest = jnp.maximum(highest, newest)
+            weights = jnp.exp2((scores - newest) * rate)
+            total = jnp.sum(weights, axis=0, keepdims=True)
+            update = lax.dot_general(
+                values[:, lanes],
+                weights.astype(jnp.bfloat16),
+                TALL,
+                preferred_element_type=jnp.float32,
+            )
+            if not first:
+                factor = jnp.exp2((highest - newest) * rate)
+                total = total + total_ref[g] * factor
+                update = update + acc_ref[g] * factor
+            high_ref[g] = newest
+            total_ref[g] = total
+            acc_ref[g] = update
+
+    shape = (capacity, stacked)
+    key_index = lax.broadcasted_iota(jnp.int32, shape, 0)
+    query_index = lax.rem(lax.broadcasted_iota(jnp.int32, shape, 1), capacity)
+
+    for copy in local_copies:
+        copy.wait()
+    attend(
+        k_buf[me],
+        v_buf[me],
+        (key_index <= query_index) & (key_index < my_count),
+        True,
+    )
+
+    def live(piece):
+        limit = jnp.broadcast_to(count_buf[piece][:, :1], shape)
+        return key_index < limit
+
+    @pl.when(column == 1)
+    def _():
+        await_piece(me - 1, (2, 0, 1))
+        attend(k_buf[me - 1], v_buf[me - 1], live(me - 1), False)
+
+    token_shape = (out_ref.shape[0], capacity)
+    chosen = (lax.broadcasted_iota(jnp.int32, token_shape, 0) == pos_ref[...]) & (
+        lax.broadcasted_iota(jnp.int32, token_shape, 1) < my_count
+    )
+
+    def fold_row(back):
+        low = WIDTH * (row - back)
+        await_piece(beside - WIDTH * back, (2, 0, 1))
+        attend(
+            k_buf[pl.ds(low, WIDTH)].reshape(WIDTH * capacity, groups * HD),
+            v_buf[pl.ds(low, WIDTH)].reshape(WIDTH * capacity, groups * HD),
+            jnp.concatenate([live(low + i) for i in range(WIDTH)], axis=0),
+            False,
+        )
+
+    for back in range(1, rows + 1):
+        if back < rows:
+
+            @pl.when(row >= back)
+            def _(back=back):
+                for kinds in ((2, 0), (1,)):
+                    await_piece(me - WIDTH * back, kinds)
+                    send_piece(kinds, back, lambda copy: copy.start())
+
+        if back > 1:
+
+            @pl.when(row >= back - 1)
+            def _(back=back):
+                fold_row(back - 1)
+
+    squares = jnp.zeros((capacity, HD), jnp.float32)
+    for g in range(groups):
+        attended = (acc_ref[g] / total_ref[g]).T.astype(jnp.bfloat16)
+        for h in range(heads):
+            one = attended[h * capacity : (h + 1) * capacity]
+            att_ref[:, (g * heads + h) * HD : (g * heads + h + 1) * HD] = one
+            wide = one.astype(jnp.float32)
+            squares = squares + wide * wide
+    square_row = lax.dot_general(
+        jnp.ones((8, HD), jnp.float32),
+        squares,
+        FLAT,
+        precision=lax.Precision.HIGHEST,
+        preferred_element_type=jnp.float32,
+    )
+    square_out[:, :capacity] = square_row
+    tp_copies = []
+    for step in range(1, tp_size):
+        tp_copies.append(
+            pltpu.make_async_remote_copy(
+                src_ref=square_out,
+                dst_ref=square_in.at[step - 1],
+                send_sem=tp_send_sem.at[step - 1],
+                recv_sem=tp_recv_sem.at[step - 1],
+                device_id={"tp": lax.rem(tp_me + step, tp_size)},
+                device_id_type=MESH,
+            )
+        )
+    for copy in tp_copies:
+        copy.start()
+
+    placed_ref[...] = (
+        jnp.dot(
+            chosen.astype(jnp.float32).astype(jnp.bfloat16),
+            att_ref[...],
+            preferred_element_type=jnp.float32,
+        )
+        * gain_ref[...]
+    )
+    for copy in tp_copies:
+        copy.wait()
+    all_squares = square_row[:1]
+    for step in range(1, tp_size):
+        all_squares = all_squares + square_in[step - 1][:1, :capacity]
+    inverse = lax.rsqrt(all_squares / (att_ref.shape[1] * tp_size) + epsilon)
+    scale = jnp.sum(
+        jnp.where(chosen, prob_ref[...] * inverse, 0.0), axis=1, keepdims=True
+    )
+    out_ref[...] = (placed_ref[...] * scale).astype(jnp.bfloat16)
+
+    for back in range(rows):
+        if back == 0:
+            send_piece((2, 0, 1), 0, lambda copy: copy.wait_send())
+        else:
+
+            @pl.when(row >= back)
+            def _(back=back):
+                send_piece((2, 0, 1), back, lambda copy: copy.wait_send())
+
+
+def local_kernel(queries, keys, values, router_prob, norm_gain, slot_pos, live_count):
+    shards, tp_size = lax.axis_size("seq"), lax.axis_size("tp")
+    capacity, width = queries.shape
+    kv_width = keys.shape[1]
+    groups = kv_width // HD
+    stacked = width // kv_width * capacity
+    rows = shards // WIDTH
+    whole = pl.BlockSpec(memory_space=pltpu.VMEM)
+    anywhere = pl.BlockSpec(memory_space=pl.ANY)
+    return pl.pallas_call(
+        functools.partial(kernel, shards, tp_size),
+        out_shape=jax.ShapeDtypeStruct((TOK_DEV, width), jnp.bfloat16),
+        in_specs=[
+            anywhere,
+            anywhere,
+            anywhere,
+            whole,
+            whole,
+            whole,
+            pl.BlockSpec(memory_space=pltpu.SMEM),
+        ],
+        out_specs=whole,
+        scratch_shapes=[
+            pltpu.VMEM((groups, stacked, HD), jnp.bfloat16),
+            pltpu.VMEM((shards, capacity, kv_width), jnp.bfloat16),
+            pltpu.VMEM((shards, capacity, kv_width), jnp.bfloat16),
+            pltpu.VMEM((shards, 1, HD), jnp.int32),
+            pltpu.VMEM((groups, 1, stacked), jnp.float32),
+            pltpu.VMEM((groups, 1, stacked), jnp.float32),
+            pltpu.VMEM((groups, HD, stacked), jnp.float32),
+            pltpu.VMEM((capacity, width), jnp.bfloat16),
+            pltpu.VMEM((TOK_DEV, width), jnp.float32),
+            pltpu.VMEM((8, 128), jnp.float32),
+            pltpu.VMEM((tp_size, 8, 128), jnp.float32),
+            pltpu.SemaphoreType.DMA((2 + width // HD,)),
+            pltpu.SemaphoreType.DMA((2, rows, 3)),
+            pltpu.SemaphoreType.DMA((shards, 3)),
+            pltpu.SemaphoreType.DMA((tp_size,)),
+            pltpu.SemaphoreType.DMA((tp_size,)),
+        ],
+        compiler_params=pltpu.CompilerParams(collective_id=0, has_side_effects=True),
+    )(
+        queries,
+        keys,
+        values,
+        router_prob.reshape(1, -1),
+        norm_gain.reshape(1, -1),
+        slot_pos.reshape(1, -1),
+        live_count,
+    )
+
+
 def solution(mesh):
     in_specs = (
         P("seq", "tp"),
@@ -156,4 +474,7 @@
         P("seq"),
     )
     out_specs = P("seq", "tp")
-    return jax.shard_map(local, mesh=mesh, in_specs=in_specs, out_specs=out_specs, check_vma=False)
+    shards = mesh.shape["seq"]
+    one_kernel = shards % WIDTH == 0 and shards <= KERNEL_SHARDS
+    body = local_kernel if one_kernel else local
+    return jax.shard_map(body, mesh=mesh, in_specs=in_specs, out_specs=out_specs, check_vma=False)

time: 98.4 us -> 24.7 us (0.25)
  the two profiles are of different devices: /device:TPU:0 before, /device:TPU:25 now
where the time goes in v1:
time: 24.7 us; the launch traced here: 24.5 us
  Pallas kernels  22 us (89%)
  local copies, waits for them, and re-layouts  1.87 us (8%)
  between operations  0.66 us (3%)
    pallas_call x1, Pallas kernels, local_kernel(): pl.pallas_call(functools.partial(kernel, shards, tp_size), out_shape=jax....  22 us
    unnamed x1, local copies, waits for them, and re-layouts  1.87 us

profile of v1, /device:TPU:25, one launch (start us, length us, event | category | flops | bytes accessed | tf_op | source)
XLA Modules:
  0.0 24.5 jit_solution(1102727095305948755)
XLA Ops:
  0.7 22.0 %shard_map.73 = bf16[256,1024]{1,0:T(8,128)(2,1)} custom-call(bf16[96,1024]{1,0:T(8,128)(2,1)} %q_hbm.1, bf16[96,256]{1,0:T(8,128)(2,1)} %k_hbm.1, bf16[96,256]{1,0:T(8,128)(2,1)} %v_hbm.1, f32[1,96]{1,0:T(1,128)} %bitcast.4, f32[1,1024]{1,0:T(1,128)} %bitcast.3, s32[1,96]{1,0:T(1,128)} %bitcast.5, s32[1]{0:T(128)S(6)} %copy.9.count_ref), custom_call_target="tpu_custom_call" | custom-call | tf_op jit(solution)/shard_map/pallas_call | solution.py:423
  22.7 1.9 %copy.10 = bf16[256,1024]{1,0:T(8,128)(2,1)} copy(bf16[256,1024]{1,0:T(8,128)(2,1)} %shard_map.73) | data formatting | bytes 1048576

commit v2 on v1

--- a/solution.py
+++ b/solution.py
@@ -149,6 +149,9 @@
 
 
 WIDTH = 2
+CHUNKS = 1
+VMEM_BYTES = 16 << 20
+ROW_BLOCKS = 1
 KERNEL_SHARDS = 16
 MESH = pl.DeviceIdType.MESH
 FLAT = (((1,), (1,)), ((), ()))
@@ -161,11 +164,10 @@
     q_hbm,
     k_hbm,
     v_hbm,
-    prob_ref,
-    gain_ref,
-    pos_ref,
-    count_ref,
-    out_ref,
+    prob_hbm,
+    count_hbm,
+    att_ref,
+    scale_ref,
     q_buf,
     k_buf,
     v_buf,
@@ -173,10 +175,10 @@
     high_ref,
     total_ref,
     acc_ref,
-    att_ref,
-    placed_ref,
     square_out,
     square_in,
+    prob_ref,
+    count_ref,
     local_sem,
     send_sem,
     recv_sem,
@@ -193,9 +195,14 @@
     heads = stacked // capacity
     rate = math.log2(math.e) / math.sqrt(HD)
 
+    count_copy = pltpu.make_async_copy(count_hbm, count_ref, local_sem.at[0])
+    count_copy.start()
+    small_copies = [
+        pltpu.make_async_copy(prob_hbm, prob_ref, local_sem.at[1]),
+    ]
     local_copies = [
-        pltpu.make_async_copy(k_hbm, k_buf.at[me], local_sem.at[0]),
-        pltpu.make_async_copy(v_hbm, v_buf.at[me], local_sem.at[1]),
+        pltpu.make_async_copy(k_hbm, k_buf.at[me], local_sem.at[4]),
+        pltpu.make_async_copy(v_hbm, v_buf.at[me], local_sem.at[5]),
     ]
     for g in range(groups):
         for h in range(heads):
@@ -203,74 +210,98 @@
                 pltpu.make_async_copy(
                     q_hbm.at[:, pl.ds((g * heads + h) * HD, HD)],
                     q_buf.at[g, pl.ds(h * capacity, capacity), :],
-                    local_sem.at[2 + g * heads + h],
+                    local_sem.at[6 + g * heads + h],
                 )
             )
-    for copy in local_copies:
+
+    barrier = pltpu.get_barrier_semaphore()
+
+    def greet(**where):
+        pl.semaphore_signal(barrier, inc=1, device_id=where, device_id_type=MESH)
+
+    greet(seq=beside)
+    for step in range(1, tp_size):
+        greet(tp=lax.rem(tp_me + step, tp_size))
+
+    met = tp_size
+    for hop in range(1, rows, 2):
+
+        @pl.when(row >= hop)
+        def _(hop=hop):
+            greet(seq=me - WIDTH * hop)
+
+        @pl.when(row < rows - hop)
+        def _(hop=hop):
+            greet(seq=me + WIDTH * hop)
+
+        met = met + jnp.where(row >= hop, 1, 0) + jnp.where(row < rows - hop, 1, 0)
+
+    for copy in local_copies + small_copies:
         copy.start()
+    count_copy.wait()
     my_count = count_ref[0]
     count_buf[me] = jnp.full(count_buf.shape[1:], my_count, jnp.int32)
     square_out[...] = jnp.zeros_like(square_out)
-
-    barrier = pltpu.get_barrier_semaphore()
-
-    def greet(**where):
-        pl.semaphore_signal(barrier, inc=1, device_id=where, device_id_type=MESH)
-
-    greet(seq=beside)
-    for step in range(1, tp_size):
-        greet(tp=lax.rem(tp_me + step, tp_size))
-
-    @pl.when(row > 0)
-    def _():
-        greet(seq=me - WIDTH)
-
-    @pl.when(row < rows - 1)
-    def _():
-        greet(seq=me + WIDTH)
-
-    pl.semaphore_wait(
-        barrier,
-        tp_size + jnp.where(row > 0, 1, 0) + jnp.where(row < rows - 1, 1, 0),
-    )
-
-    def piece_copy(kind, piece, way, back):
-        buffer = (k_buf, v_buf, count_buf)[kind]
-        source = buffer.at[piece]
-        if back == 0 and kind < 2:
-            source = (k_hbm, v_hbm)[kind]
+    pl.semaphore_wait(barrier, met)
+
+    length = capacity // CHUNKS
+    parts = [(count_buf, None, slice(0, 1))]
+    for buffer, own in ((k_buf, k_hbm), (v_buf, v_hbm)):
+        for chunk in range(CHUNKS):
+            parts.append((buffer, own, pl.ds(chunk * length, length)))
+
+    def part_copy(part, piece, hop, back):
+        buffer, own, span = parts[part]
+        target = buffer.at[piece, span]
+        source = target
         return pltpu.make_async_remote_copy(
             src_ref=source,
-            dst_ref=buffer.at[piece],
-            send_sem=send_sem.at[way, back, kind],
-            recv_sem=recv_sem.at[piece, kind],
-            device_id={"seq": (me + WIDTH, beside)[way]},
+            dst_ref=target,
+            send_sem=send_sem.at[hop, back, part],
+            recv_sem=recv_sem.at[piece, part],
+            device_id={"seq": me + WIDTH * hop if hop else beside},
             device_id_type=MESH,
         )
 
-    def send_piece(kinds, back, act):
-        piece = me - WIDTH * back
-
-        @pl.when(row < rows - 1)
-        def _():
-            for kind in kinds:
-                act(piece_copy(kind, piece, 0, back))
-
+    def each_target(back, act):
+        hops = range(1, rows, 2) if back == 0 else (1,) if back % 2 else ()
+        for hop in hops:
+
+            @pl.when(row < rows - hop)
+            def _(hop=hop):
+                act(hop)
+
+            if hop == 1:
+                each_beside(back, act)
+        if not hops:
+            each_beside(back, act)
+
+    def each_beside(back, act):
         if back == 0:
 
             @pl.when(column == 0)
             def _():
-                for kind in kinds:
-                    act(piece_copy(kind, piece, 1, back))
+                act(0)
         else:
-            for kind in kinds:
-                act(piece_copy(kind, piece, 1, back))
-
-    def await_piece(piece, kinds):
-        for kind in kinds:
-            piece_copy(kind, piece, 0, 1).wait_recv()
-
-    send_piece((2, 0, 1), 0, lambda copy: copy.start())
+            act(0)
+
+    def await_piece(piece):
+        for part in range(len(parts)):
+            part_copy(part, piece, 0, 1).wait_recv()
+
+    def send_own(hop):
+        for part in range(len(parts)):
+            part_copy(part, me, hop, 0).start()
+
+    for copy in local_copies[:2]:
+        copy.wait()
+    each_target(0, send_own)
+
+    def relay(back):
+        piece = me - WIDTH * back
+        for part in range(len(parts)):
+            part_copy(part, piece, 0, 1).wait_recv()
+            each_target(back, lambda hop: part_copy(part, piece, hop, back).start())
 
     def attend(keys, values, visible, first):
         for g in range(groups):
@@ -303,7 +334,7 @@
     key_index = lax.broadcasted_iota(jnp.int32, shape, 0)
     query_index = lax.rem(lax.broadcasted_iota(jnp.int32, shape, 1), capacity)
 
-    for copy in local_copies:
+    for copy in local_copies[2:]:
         copy.wait()
     attend(
         k_buf[me],
@@ -316,19 +347,18 @@
         limit = jnp.broadcast_to(count_buf[piece][:, :1], shape)
         return key_index < limit
 
-    @pl.when(column == 1)
-    def _():
-        await_piece(me - 1, (2, 0, 1))
-        attend(k_buf[me - 1], v_buf[me - 1], live(me - 1), False)
-
-    token_shape = (out_ref.shape[0], capacity)
-    chosen = (lax.broadcasted_iota(jnp.int32, token_shape, 0) == pos_ref[...]) & (
-        lax.broadcasted_iota(jnp.int32, token_shape, 1) < my_count
-    )
+    def fold_beside():
+        @pl.when(column == 1)
+        def _():
+            await_piece(me - 1)
+            attend(k_buf[me - 1], v_buf[me - 1], live(me - 1), False)
+
+    for copy in small_copies:
+        copy.wait()
 
     def fold_row(back):
         low = WIDTH * (row - back)
-        await_piece(beside - WIDTH * back, (2, 0, 1))
+        await_piece(beside - WIDTH * back)
         attend(
             k_buf[pl.ds(low, WIDTH)].reshape(WIDTH * capacity, groups * HD),
             v_buf[pl.ds(low, WIDTH)].reshape(WIDTH * capacity, groups * HD),
@@ -341,11 +371,11 @@
 
             @pl.when(row >= back)
             def _(back=back):
-                for kinds in ((2, 0), (1,)):
-                    await_piece(me - WIDTH * back, kinds)
-                    send_piece(kinds, back, lambda copy: copy.start())
-
-        if back > 1:
+                relay(back)
+
+        if back == 1:
+            fold_beside()
+        else:
 
             @pl.when(row >= back - 1)
             def _(back=back):
@@ -382,33 +412,46 @@
     for copy in tp_copies:
         copy.start()
 
-    placed_ref[...] = (
-        jnp.dot(
-            chosen.astype(jnp.float32).astype(jnp.bfloat16),
-            att_ref[...],
-            preferred_element_type=jnp.float32,
-        )
-        * gain_ref[...]
-    )
     for copy in tp_copies:
         copy.wait()
     all_squares = square_row[:1]
     for step in range(1, tp_size):
         all_squares = all_squares + square_in[step - 1][:1, :capacity]
     inverse = lax.rsqrt(all_squares / (att_ref.shape[1] * tp_size) + epsilon)
+    scale_ref[:, :capacity] = jnp.broadcast_to(
+        prob_ref[...] * inverse, (scale_ref.shape[0], capacity)
+    )
+
+    def settle(back):
+        def wait(hop):
+            for part in range(len(parts)):
+                part_copy(part, me - WIDTH * back, hop, back).wait_send()
+
+        each_target(back, wait)
+
+    settle(0)
+    for back in range(1, rows):
+
+        @pl.when(row >= back)
+        def _(back=back):
+            settle(back)
+
+
+def place_kernel(att_ref, scale_ref, gain_ref, pos_ref, count_ref, out_ref):
+    shape = (out_ref.shape[0], att_ref.shape[0])
+    first = pl.program_id(0) * shape[0]
+    chosen = (lax.broadcasted_iota(jnp.int32, shape, 0) + first == pos_ref[...]) & (
+        lax.broadcasted_iota(jnp.int32, shape, 1) < count_ref[0]
+    )
+    placed = jnp.dot(
+        chosen.astype(jnp.float32).astype(jnp.bfloat16),
+        att_ref[...],
+        preferred_element_type=jnp.float32,
+    )
     scale = jnp.sum(
-        jnp.where(chosen, prob_ref[...] * inverse, 0.0), axis=1, keepdims=True
-    )
-    out_ref[...] = (placed_ref[...] * scale).astype(jnp.bfloat16)
-
-    for back in range(rows):
-        if back == 0:
-            send_piece((2, 0, 1), 0, lambda copy: copy.wait_send())
-        else:
-
-            @pl.when(row >= back)
-            def _(back=back):
-                send_piece((2, 0, 1), back, lambda copy: copy.wait_send())
+        jnp.where(chosen, scale_ref[:1, : shape[1]], 0.0), axis=1, keepdims=True
+    )
+    out_ref[...] = (placed * gain_ref[...] * scale).astype(jnp.bfloat16)
 
 
 def local_kernel(queries, keys, values, router_prob, norm_gain, slot_pos, live_count):
@@ -419,20 +462,21 @@
     stacked = width // kv_width * capacity
     rows = shards // WIDTH
     whole = pl.BlockSpec(memory_space=pltpu.VMEM)
-    anywhere = pl.BlockSpec(memory_space=pl.ANY)
-    return pl.pallas_call(
+    anywhere = pl.BlockSpec(memory_space=pltpu.HBM)
+    attended, scale = pl.pallas_call(
         functools.partial(kernel, shards, tp_size),
-        out_shape=jax.ShapeDtypeStruct((TOK_DEV, width), jnp.bfloat16),
+        out_shape=(
+            pltpu.VMEM((capacity, width), jnp.bfloat16),
+            pltpu.VMEM((8, 128), jnp.float32),
+        ),
         in_specs=[
             anywhere,
             anywhere,
             anywhere,
-            whole,
-            whole,
-            whole,
-            pl.BlockSpec(memory_space=pltpu.SMEM),
+            anywhere,
+            anywhere,
         ],
-        out_specs=whole,
+        out_specs=(whole, whole),
         scratch_shapes=[
             pltpu.VMEM((groups, stacked, HD), jnp.bfloat16),
             pltpu.VMEM((shards, capacity, kv_width), jnp.bfloat16),
@@ -441,26 +485,42 @@
             pltpu.VMEM((groups, 1, stacked), jnp.float32),
             pltpu.VMEM((groups, 1, stacked), jnp.float32),
             pltpu.VMEM((groups, HD, stacked), jnp.float32),
-            pltpu.VMEM((capacity, width), jnp.bfloat16),
-            pltpu.VMEM((TOK_DEV, width), jnp.float32),
             pltpu.VMEM((8, 128), jnp.float32),
             pltpu.VMEM((tp_size, 8, 128), jnp.float32),
-            pltpu.SemaphoreType.DMA((2 + width // HD,)),
-            pltpu.SemaphoreType.DMA((2, rows, 3)),
-            pltpu.SemaphoreType.DMA((shards, 3)),
+            pltpu.VMEM((1, capacity), jnp.float32),
+            pltpu.SMEM((1,), jnp.int32),
+            pltpu.SemaphoreType.DMA((6 + width // HD,)),
+            pltpu.SemaphoreType.DMA((rows, rows, 1 + 2 * CHUNKS)),
+            pltpu.SemaphoreType.DMA((shards, 1 + 2 * CHUNKS)),
             pltpu.SemaphoreType.DMA((tp_size,)),
             pltpu.SemaphoreType.DMA((tp_size,)),
         ],
-        compiler_params=pltpu.CompilerParams(collective_id=0, has_side_effects=True),
+        compiler_params=pltpu.CompilerParams(
+            collective_id=0, has_side_effects=True
+        ),
     )(
         queries,
         keys,
         values,
         router_prob.reshape(1, -1),
-        norm_gain.reshape(1, -1),
-        slot_pos.reshape(1, -1),
         live_count,
     )
+    block = TOK_DEV // ROW_BLOCKS
+    return pl.pallas_call(
+        place_kernel,
+        grid=(ROW_BLOCKS,),
+        out_shape=jax.ShapeDtypeStruct((TOK_DEV, width), jnp.bfloat16),
+        in_specs=[
+            whole,
+            whole,
+            whole,
+            whole,
+            pl.BlockSpec(memory_space=pltpu.SMEM),
+        ],
+        out_specs=pl.BlockSpec((block, width), lambda i: (i, 0)),
+        compiler_params=pltpu.CompilerParams(vmem_limit_bytes=VMEM_BYTES),
+        name="place",
+    )(attended, scale, norm_gain.reshape(1, -1), slot_pos.reshape(1, -1), live_count)
 
 
 def solution(mesh):

time: 24.7 us -> 21.6 us (0.87)
  Pallas kernels: 22 us -> 20.1 us
  local copies, waits for them, and re-layouts: 1.87 us -> 0.64 us
    pallas_call x1 -> x2, Pallas kernels: 22 us -> 20.1 us  [the longest x1 19 us: local_kernel(): pl.pallas_call(functools.partial(kernel, shards, tp_size), out_shape=(plt...]
    unnamed x1 -> x4, local copies, waits for them, and re-layouts: 1.87 us -> 0.64 us
where the time goes in v2:
time: 21.6 us; the launch traced here: 21.4 us
  Pallas kernels  20.1 us (93%)
  between operations  0.68 us (3%)
  local copies, waits for them, and re-layouts  0.64 us (3%)
    pallas_call x1, Pallas kernels, local_kernel(): pl.pallas_call(functools.partial(kernel, shards, tp_size), out_shape=(plt...  19 us
    pallas_call x1, Pallas kernels, local_kernel(): pl.pallas_call(place_kernel, grid=(ROW_BLOCKS,), out_shape=jax.ShapeDtype...  1.08 us
    unnamed x4, local copies, waits for them, and re-layouts  0.64 us

profile of v2, /device:TPU:25, one launch (start us, length us, event | category | flops | bytes accessed | tf_op | source)
XLA Modules:
  0.0 21.4 jit_solution(1232270048871404181)
XLA Ops:
  0.7 0.0 copy-start
  0.7 19.0 %shard_map.73 = (bf16[96,1024]{1,0:T(8,128)(2,1)S(1)}, f32[8,128]{1,0:T(8,128)S(1)}) custom-call(bf16[96,1024]{1,0:T(8,128)(2,1)} %q_hbm.1, bf16[96,256]{1,0:T(8,128)(2,1)} %k_hbm.1, bf16[96,256]{1,0:T(8,128)(2,1)} %v_hbm.1, f32[1,96]{1,0:T(1,128)} %bitcast.5, s32[1]{0:T(128)S(6)} %copy.8.count_hbm.count_ref), custom_call_target="tpu_custom_call" | custom-call | tf_op jit(solution)/shard_map/pallas_call | solution.py:466
  19.7 0.0 copy-start.1
  19.7 0.0 copy-done
  19.7 0.6 %copy-done.1 = s32[96]{0:T(128)S(1)} copy-done((s32[96]{0:T(128)S(1)}, s32[96]{0:T(128)}, u32[]{:S(2)}) %copy-start.1) | copy-done | bytes 408
  20.3 1.1 %place.1 = bf16[256,1024]{1,0:T(8,128)(2,1)} custom-call(bf16[96,1024]{1,0:T(8,128)(2,1)S(1)} %get-tuple-element.7.att_ref, f32[8,128]{1,0:T(8,128)S(1)} %get-tuple-element.8.scale_ref, f32[1,1024]{1,0:T(1,128)S(1)} %bitcast.3, s32[1,96]{1,0:T(1,128)S(1)} %bitcast.4, s32[1]{0:T(128)S(6)} %copy.8.count_hbm.count_ref), custom_call_target="tpu_custom_call" | custom-call | tf_op jit(solution)/shard_map/place/pallas_call | solution.py:509
Async XLA Ops:
  0.7 19.0 %copy-start = (f32[1024]{0:T(1024)S(1)}, f32[1024]{0:T(1024)}, u32[]{:S(2)}) copy-start(f32[1024]{0:T(1024)} %param.11) | copy-start | bytes 12292
  19.7 0.7 %copy-start.1 = (s32[96]{0:T(128)S(1)}, s32[96]{0:T(128)}, u32[]{:S(2)}) copy-start(s32[96]{0:T(128)} %param.12) | copy-start | bytes 1156

commit v3 on v2

--- a/solution.py
+++ b/solution.py
@@ -224,7 +224,7 @@
         greet(tp=lax.rem(tp_me + step, tp_size))
 
     met = tp_size
-    for hop in range(1, rows, 2):
+    for hop in (1,):
 
         @pl.when(row >= hop)
         def _(hop=hop):
@@ -264,7 +264,7 @@
         )
 
     def each_target(back, act):
-        hops = range(1, rows, 2) if back == 0 else (1,) if back % 2 else ()
+        hops = (1,) if back == 0 else (1,)
         for hop in hops:
 
             @pl.when(row < rows - hop)

time: 21.6 us -> 21.1 us (0.977)
  Pallas kernels: 20.1 us -> 19.6 us
    pallas_call x1, Pallas kernels: 19 us -> 18.6 us  [local_kernel(): pl.pallas_call(functools.partial(kernel, shards, tp_size), out_shape=(plt...]
where the time goes in v3:
time: 21.1 us; the launch traced here: 21 us
  Pallas kernels  19.6 us (93%)
  between operations  0.68 us (3%)
  local copies, waits for them, and re-layouts  0.64 us (3%)
    pallas_call x1, Pallas kernels, local_kernel(): pl.pallas_call(functools.partial(kernel, shards, tp_size), out_shape=(plt...  18.6 us
    pallas_call x1, Pallas kernels, local_kernel(): pl.pallas_call(place_kernel, grid=(ROW_BLOCKS,), out_shape=jax.ShapeDtype...  1.08 us
    unnamed x4, local copies, waits for them, and re-layouts  0.64 us

profile of v3, /device:TPU:25, one launch (start us, length us, event | category | flops | bytes accessed | tf_op | source)
XLA Modules:
  0.0 21.0 jit_solution(18344915391183979956)
XLA Ops:
  0.7 0.0 copy-start
  0.7 18.6 %shard_map.73 = (bf16[96,1024]{1,0:T(8,128)(2,1)S(1)}, f32[8,128]{1,0:T(8,128)S(1)}) custom-call(bf16[96,1024]{1,0:T(8,128)(2,1)} %q_hbm.1, bf16[96,256]{1,0:T(8,128)(2,1)} %k_hbm.1, bf16[96,256]{1,0:T(8,128)(2,1)} %v_hbm.1, f32[1,96]{1,0:T(1,128)} %bitcast.5, s32[1]{0:T(128)S(6)} %copy.8.count_hbm.count_ref), custom_call_target="tpu_custom_call" | custom-call | tf_op jit(solution)/shard_map/pallas_call | solution.py:466
  19.2 0.0 copy-start.1
  19.2 0.0 copy-done
  19.2 0.6 %copy-done.1 = s32[96]{0:T(128)S(1)} copy-done((s32[96]{0:T(128)S(1)}, s32[96]{0:T(128)}, u32[]{:S(2)}) %copy-start.1) | copy-done | bytes 408
  19.9 1.1 %place.1 = bf16[256,1024]{1,0:T(8,128)(2,1)} custom-call(bf16[96,1024]{1,0:T(8,128)(2,1)S(1)} %get-tuple-element.7.att_ref, f32[8,128]{1,0:T(8,128)S(1)} %get-tuple-element.8.scale_ref, f32[1,1024]{1,0:T(1,128)S(1)} %bitcast.3, s32[1,96]{1,0:T(1,128)S(1)} %bitcast.4, s32[1]{0:T(128)S(6)} %copy.8.count_hbm.count_ref), custom_call_target="tpu_custom_call" | custom-call | tf_op jit(solution)/shard_map/place/pallas_call | solution.py:509
Async XLA Ops:
  0.7 18.6 %copy-start = (f32[1024]{0:T(1024)S(1)}, f32[1024]{0:T(1024)}, u32[]{:S(2)}) copy-start(f32[1024]{0:T(1024)} %param.11) | copy-start | bytes 12292
  19.2 0.7 %copy-start.1 = (s32[96]{0:T(128)S(1)}, s32[96]{0:T(128)}, u32[]{:S(2)}) copy-start(s32[96]{0:T(128)} %param.12) | copy-start | bytes 1156

commit v4 on v3

--- a/solution.py
+++ b/solution.py
@@ -214,6 +214,9 @@
                 )
             )
 
+    for copy in local_copies + small_copies:
+        copy.start()
+
     barrier = pltpu.get_barrier_semaphore()
 
     def greet(**where):
@@ -224,20 +227,18 @@
         greet(tp=lax.rem(tp_me + step, tp_size))
 
     met = tp_size
-    for hop in (1,):
-
-        @pl.when(row >= hop)
-        def _(hop=hop):
-            greet(seq=me - WIDTH * hop)
-
-        @pl.when(row < rows - hop)
-        def _(hop=hop):
-            greet(seq=me + WIDTH * hop)
-
-        met = met + jnp.where(row >= hop, 1, 0) + jnp.where(row < rows - hop, 1, 0)
-
-    for copy in local_copies + small_copies:
-        copy.start()
+    @pl.when(row > 0)
+    def _():
+        greet(seq=me - WIDTH)
+        greet(seq=beside - WIDTH)
+
+    @pl.when(row < rows - 1)
+    def _():
+        greet(seq=me + WIDTH)
+        greet(seq=beside + WIDTH)
+
+    met = met + jnp.where(row > 0, 2, 0) + jnp.where(row < rows - 1, 2, 0)
+
     count_copy.wait()
     my_count = count_ref[0]
     count_buf[me] = jnp.full(count_buf.shape[1:], my_count, jnp.int32)
@@ -259,31 +260,29 @@
             dst_ref=target,
             send_sem=send_sem.at[hop, back, part],
             recv_sem=recv_sem.at[piece, part],
-            device_id={"seq": me + WIDTH * hop if hop else beside},
+            device_id={"seq": (beside, me + WIDTH, beside + WIDTH)[hop]},
             device_id_type=MESH,
         )
 
     def each_target(back, act):
-        hops = (1,) if back == 0 else (1,)
-        for hop in hops:
-
-            @pl.when(row < rows - hop)
-            def _(hop=hop):
-                act(hop)
-
-            if hop == 1:
-                each_beside(back, act)
-        if not hops:
-            each_beside(back, act)
-
-    def each_beside(back, act):
+        @pl.when(row < rows - 1)
+        def _():
+            act(1)
+
+        @pl.when((row < rows - 1) & (row == back))
+        def _():
+            act(2)
+
         if back == 0:
 
             @pl.when(column == 0)
             def _():
                 act(0)
         else:
-            act(0)
+
+            @pl.when(row != back)
+            def _():
+                act(0)
 
     def await_piece(piece):
         for part in range(len(parts)):
@@ -490,7 +489,7 @@
             pltpu.VMEM((1, capacity), jnp.float32),
             pltpu.SMEM((1,), jnp.int32),
             pltpu.SemaphoreType.DMA((6 + width // HD,)),
-            pltpu.SemaphoreType.DMA((rows, rows, 1 + 2 * CHUNKS)),
+            pltpu.SemaphoreType.DMA((3, rows, 1 + 2 * CHUNKS)),
             pltpu.SemaphoreType.DMA((shards, 1 + 2 * CHUNKS)),
             pltpu.SemaphoreType.DMA((tp_size,)),
             pltpu.SemaphoreType.DMA((tp_size,)),

time: 21.1 us -> 20.9 us (level)
  the two profiles are of different devices: /device:TPU:25 before, /device:TPU:29 now
where the time goes in v4:
time: 20.9 us; the launch traced here: 20.7 us
  Pallas kernels  19.4 us (93%)
  between operations  0.68 us (3%)
  local copies, waits for them, and re-layouts  0.64 us (3%)
    pallas_call x1, Pallas kernels, local_kernel(): pl.pallas_call(functools.partial(kernel, shards, tp_size), out_shape=(plt...  18.3 us
    pallas_call x1, Pallas kernels, local_kernel(): pl.pallas_call(place_kernel, grid=(ROW_BLOCKS,), out_shape=jax.ShapeDtype...  1.08 us
    unnamed x4, local copies, waits for them, and re-layouts  0.64 us

profile of v4, /device:TPU:29, one launch (start us, length us, event | category | flops | bytes accessed | tf_op | source)
XLA Modules:
  0.0 20.7 jit_solution(2990220885450126493)
XLA Ops:
  0.7 0.0 copy-start
  0.7 18.3 %shard_map.73 = (bf16[96,1024]{1,0:T(8,128)(2,1)S(1)}, f32[8,128]{1,0:T(8,128)S(1)}) custom-call(bf16[96,1024]{1,0:T(8,128)(2,1)} %q_hbm.1, bf16[96,256]{1,0:T(8,128)(2,1)} %k_hbm.1, bf16[96,256]{1,0:T(8,128)(2,1)} %v_hbm.1, f32[1,96]{1,0:T(1,128)} %bitcast.5, s32[1]{0:T(128)S(6)} %copy.8.count_hbm.count_ref), custom_call_target="tpu_custom_call" | custom-call | tf_op jit(solution)/shard_map/pallas_call | solution.py:465
  19.0 0.0 copy-start.1
  19.0 0.0 copy-done
  19.0 0.6 %copy-done.1 = s32[96]{0:T(128)S(1)} copy-done((s32[96]{0:T(128)S(1)}, s32[96]{0:T(128)}, u32[]{:S(2)}) %copy-start.1) | copy-done | bytes 408
  19.7 1.1 %place.1 = bf16[256,1024]{1,0:T(8,128)(2,1)} custom-call(bf16[96,1024]{1,0:T(8,128)(2,1)S(1)} %get-tuple-element.7.att_ref, f32[8,128]{1,0:T(8,128)S(1)} %get-tuple-element.8.scale_ref, f32[1,1024]{1,0:T(1,128)S(1)} %bitcast.3, s32[1,96]{1,0:T(1,128)S(1)} %bitcast.4, s32[1]{0:T(128)S(6)} %copy.8.count_hbm.count_ref), custom_call_target="tpu_custom_call" | custom-call | tf_op jit(solution)/shard_map/place/pallas_call | solution.py:508
Async XLA Ops:
  0.7 18.4 %copy-start = (f32[1024]{0:T(1024)S(1)}, f32[1024]{0:T(1024)}, u32[]{:S(2)}) copy-start(f32[1024]{0:T(1024)} %param.11) | copy-start | bytes 12292
  19.0 0.7 %copy-start.1 = (s32[96]{0:T(128)S(1)}, s32[96]{0:T(128)}, u32[]{:S(2)}) copy-start(s32[96]{0:T(128)} %param.12) | copy-start | bytes 1156
